TPU v7x, 128 devices: a whole 4x4x4 slice. The times are simulated.
128 devices in a mesh: req: 32 (over y, z, core), tp: 4 (over x).
Axes of the slice: x: 4, y: 4, z: 4, core: 2. Of those that a mesh axis runs over, the one named last changes fastest.
Arguments:
- states: bfloat16 [64, 512, 1024], P('req', 'tp'), may hold values from -45 to 45
- lengths: int32 [64], P('req'), may hold values from 3 to 512, as said below
- w_qkv: bfloat16 [1024, 3, 1024], P(None, None, 'tp'), may hold values from -0.1875 to 0.1875
- b_qkv: float32 [3, 1024], P(None, 'tp'), may hold values from -3 to 3
- w_out: bfloat16 [1024, 1024], P('tp'), may hold values from -0.1875 to 0.1875
- b_out: float32 [1024], replicated, may hold values from -3 to 3
- ln1_gain: float32 [1024], replicated, may hold values from 0.1 to 1.9
- ln1_shift: float32 [1024], replicated, may hold values from -3 to 3
- w_up: bfloat16 [1024, 4096], P(None, 'tp'), may hold values from -0.1875 to 0.1875
- b_up: float32 [4096], P('tp'), may hold values from -3 to 3
- w_down: bfloat16 [4096, 1024], P('tp'), may hold values from -0.09375 to 0.09375
- b_down: float32 [1024], replicated, may hold values from -3 to 3
- ln2_gain: float32 [1024], replicated, may hold values from 0.1 to 1.9
- ln2_shift: float32 [1024], replicated, may hold values from -3 to 3
- index_rows: bfloat16 [524288, 1024], P(('req', 'tp')), may hold values from -0.1875 to 0.1875
- cand_ids: int32 [64, 64], P('req', 'tp'), may hold values from 0 to 524287
Outputs:
- hidden_out: bfloat16 [64, 512, 1024], P('req', 'tp')
- scores: float32 [64, 64], P('req', 'tp')
Inputs may be any that keep to these rules, and one draw needn't show every extreme that they name: Valid positions are the first lengths ones of a text; in every draw some text has 512.
All inputs are finite; a program needn't handle non-finite values.
Results may differ from a plain program's by a relative error of at most 0.015.
Values may be sent and summed in bfloat16 or wider, within the bound.
A program may use at most 128 MiB of HBM per device.

v0:
```python
import jax
import jax.numpy as jnp
from jax import lax
from jax.sharding import PartitionSpec as P

HEAD_DIM = 64
WINDOW = 512
layer_eps = 1e-05
norm_eps = 1e-06


def layer_norm(values, gain, shift):
    centre = values - jnp.mean(values, axis=-1, keepdims=True)
    spread = jnp.mean(centre * centre, axis=-1, keepdims=True)
    return centre * lax.rsqrt(spread + layer_eps) * gain + shift


def window_attention(queries_h, keys_h, values_h, length):
    seq_len = queries_h.shape[0]
    half_window = WINDOW // 2
    padding = ((half_window, half_window), (0, 0), (0, 0))
    keys_padded = jnp.pad(keys_h, padding)
    values_padded = jnp.pad(values_h, padding)
    scale_factor = HEAD_DIM ** (-0.5)

    def one_block(block_idx):
        blk_start = block_idx * WINDOW
        query_pos = blk_start + jnp.arange(WINDOW, dtype=jnp.int32)
        key_pos = blk_start - half_window + jnp.arange(2 * WINDOW, dtype=jnp.int32)
        keep_mask = (
            (jnp.abs(query_pos[:, None] - key_pos[None, :]) <= half_window)
            & (key_pos[None, :] >= 0)
            & (key_pos[None, :] < length)
        )
        logits = (
            jnp.einsum("qhe,khe->hqk", queries_h, keys_padded, preferred_element_type=jnp.float32)
            * scale_factor
        )
        logits = jnp.where(keep_mask[None], logits, jnp.float32(-1e30))
        top_val = jnp.max(logits, axis=-1, keepdims=True)
        expo = jnp.exp(logits - top_val)
        attn_weights = (expo / jnp.sum(expo, axis=-1, keepdims=True)).astype(jnp.bfloat16)
        context = jnp.einsum(
            "hqk,khe->qhe", attn_weights, values_padded, preferred_element_type=jnp.float32
        )
        context = jnp.where((query_pos < length)[:, None, None], context, jnp.float32(0.0))
        return context.astype(jnp.bfloat16)

    blocks = lax.map(one_block, jnp.arange(seq_len // WINDOW, dtype=jnp.int32))
    return blocks.reshape(seq_len, queries_h.shape[1] * HEAD_DIM)


def per_device(
    states,
    lengths,
    w_qkv,
    b_qkv,
    w_out,
    b_out,
    ln1_gain,
    ln1_shift,
    w_up,
    b_up,
    w_down,
    b_down,
    ln2_gain,
    ln2_shift,
    index_rows,
    cand_ids,
):
    tp_count = lax.axis_size("tp")
    tp_rank = lax.axis_index("tp")
    req_count = lax.axis_size("req")
    text_count, row_share, model_width = states.shape
    full_states = lax.all_gather(states, "tp", axis=1, tiled=True)
    seq_len = full_states.shape[1]
    local_width = w_qkv.shape[2]
    heads_here = local_width // HEAD_DIM
    projected = (
        jnp.einsum("tsd,dce->tsce", full_states, w_qkv, preferred_element_type=jnp.float32) + b_qkv
    ).astype(jnp.bfloat16)
    queries_h = projected[:, :, 0].reshape(text_count, seq_len, heads_here, HEAD_DIM)
    keys_h = projected[:, :, 1].reshape(text_count, seq_len, heads_here, HEAD_DIM)
    values_h = projected[:, :, 2].reshape(text_count, seq_len, heads_here, HEAD_DIM)

    def per_text(bundle):
        return window_attention(bundle[0], bundle[1], bundle[2], bundle[3])

    context = lax.map(per_text, (queries_h, keys_h, values_h, lengths))
    partial_value = jnp.einsum("tsk,kd->tsd", context, w_out, preferred_element_type=jnp.float32)
    attn_sum = lax.psum(partial_value.astype(jnp.bfloat16), "tp").astype(jnp.float32)
    normed_full = layer_norm(
        full_states.astype(jnp.float32) + attn_sum + b_out, ln1_gain, ln1_shift
    ).astype(jnp.bfloat16)
    normed_local = lax.dynamic_slice_in_dim(normed_full, tp_rank * row_share, row_share, 1)
    up_act = jax.nn.gelu(
        jnp.einsum("tsd,df->tsf", normed_full, w_up, preferred_element_type=jnp.float32) + b_up,
        approximate=False,
    ).astype(jnp.bfloat16)
    down_part = jnp.einsum("tsf,fd->tsd", up_act, w_down, preferred_element_type=jnp.float32)
    down_sum = lax.psum_scatter(
        down_part.astype(jnp.bfloat16), "tp", scatter_dimension=1, tiled=True
    ).astype(jnp.float32)
    hidden_out = layer_norm(
        normed_local.astype(jnp.float32) + down_sum + b_down, ln2_gain, ln2_shift
    ).astype(jnp.bfloat16)
    positions = tp_rank * row_share + jnp.arange(row_share, dtype=jnp.int32)
    is_valid = positions[None, :] < lengths[:, None]
    local_pool = jnp.sum(
        jnp.where(is_valid[:, :, None], hidden_out.astype(jnp.float32), jnp.float32(0.0)), axis=1
    )
    pooled = lax.psum(local_pool, "tp") / lengths.astype(jnp.float32)[:, None]
    query_vec = (
        pooled * lax.rsqrt(jnp.mean(pooled * pooled, axis=-1, keepdims=True) + norm_eps)
    ).astype(jnp.bfloat16)
    all_queries = lax.all_gather(query_vec, "req", axis=0, tiled=True)
    quarter = cand_ids.shape[1]
    gathered_ids = lax.all_gather(cand_ids, ("req", "tp"), axis=0, tiled=True)
    all_ids = (
        gathered_ids.reshape(req_count, tp_count, text_count, quarter)
        .transpose(0, 2, 1, 3)
        .reshape(req_count * text_count, tp_count * quarter)
    )
    rows_here = index_rows.shape[0]
    first_row = (lax.axis_index("req") * tp_count + tp_rank) * rows_here
    local_ids = all_ids - first_row
    is_owned = (local_ids >= 0) & (local_ids < rows_here)
    safe_ids = jnp.clip(local_ids, 0, rows_here - 1)
    fetched = jnp.take(index_rows, safe_ids.reshape(-1), axis=0).reshape(
        safe_ids.shape[0], safe_ids.shape[1], model_width
    )
    picked = jnp.einsum("td,tcd->tc", all_queries, fetched, preferred_element_type=jnp.float32)
    owner_terms = jnp.where(is_owned, picked, jnp.float32(0.0))
    owner_terms = (
        owner_terms.reshape(req_count, text_count, tp_count, quarter)
        .transpose(0, 2, 1, 3)
        .reshape(req_count * tp_count * text_count, quarter)
    )
    scores = lax.psum_scatter(owner_terms, ("req", "tp"), scatter_dimension=0, tiled=True)
    return (hidden_out, scores)


def solution(mesh):
    placed = (
        P("req", "tp", None),
        P("req"),
        P(None, None, "tp"),
        P(None, "tp"),
        P("tp", None),
        P(),
        P(),
        P(),
        P(None, "tp"),
        P("tp"),
        P("tp", None),
        P(),
        P(),
        P(),
        P(("req", "tp"), None),
        P("req", "tp"),
    )
    return jax.shard_map(
        per_device,
        mesh=mesh,
        in_specs=placed,
        out_specs=(P("req", "tp", None), P("req", "tp")),
        check_vma=False,
    )
```

profile of v0, /device:TPU:1, one launch (start us, length us, event | category | flops | bytes accessed | tf_op | source)
XLA Modules:
  0.0 362.5 jit_solution(10841223569805811967)
XLA Ops:
  8.0 35.7 %all-gather.4.cloned.1.call-done = bf16[2,512,1024]{2,1,0:T(8,128)(2,1)} async-done(((bf16[2,128,1024]{2,1,0:T(8,128)(2,1)}), bf16[2,512,1024]{2,1,0:T(8,128)(2,1)}) %all-gather.4.cloned.1.call-update) | async-done | bytes 2097168 | tf_op jit(solution)/shard_map/all_gather | solution.py:75
  43.7 3.9 %add_convert_fusion.1 = bf16[2,512,3,256]{1,3,2,0:T(8,128)(2,1)S(1)} fusion(f32[3,256]{1,0:T(4,128)} %param.21, bf16[1024,3,256]{2,0,1:T(8,128)(2,1)} %param.20, bf16[2,512,1024]{2,1,0:T(8,128)(2,1)} %all-gather.4.cloned.1.call-done), kind=kOutput, calls=%fused_computation.68 | convolution fusion | flops 1612185600 | bytes 5245952 | tf_op jit(solution)/shard_map/tsd,dce->tsce/dot_general | solution.py:80
  47.6 1.2 fusion.150
  48.8 33.0 %while.17 = (s32[]{:T(128)}, bf16[2,512,256]{1,2,0:T(8,128)(2,1)}, s32[2]{0:T(128)S(1)}, bf16[2,512,4,64]{1,3,2,0:T(8,128)(2,1)}, bf16[2,512,4,64]{1,3,2,0:T(8,1...) while((s32[]{:T(128)}, bf16[2,512,256]{1,2,0:T(8,128)(2,1)}, s32[2]{0:T(128)S(1)}, ...), condition=%wide.region_3.4_spmd, body=%wide.region_0.3_spmd.sunk | while | flops 552343040 | bytes 24671904 | solution.py:89
  52.0 6.9 %fusion.166 = (f32[4,512]{1,0:T(4,128)S(1)}, f32[4,512,1024]{2,1,0:T(8,128)}) fusion(pred[512,1024]{1,0:T(8,128)(4,1)S(1)} %fusion.165, bf16[512,4,64]{0,2,1:T(8,128)(2,1)S(1)} %get-tuple-element.195, bf16[2,512,4,64]{1,3,2,0:T(8,128)(2,1)} %get-tuple-element.217, s32[]{:T(128)} %get-tuple-element.206), kind=kOutput, calls=%fused_computation.171.clone.1 | convolution fusion | flops 276825088 | bytes 9445888 | tf_op jit(solution)/shard_map/while/body/eval_jaxpr/while/body/eval_jaxpr/sub | solution.py:41
  59.6 4.9 %fusion.167 = bf16[4,64,512]{2,1,0:T(8,128)(2,1)S(1)} fusion(f32[4,512,1024]{2,1,0:T(8,128)} %get-tuple-element.196, f32[4,512]{1,0:T(4,128)S(1)} %get-tuple-element.197, bf16[512,4,64]{0,2,1:T(8,128)(2,1)S(1)} %get-tuple-element.198, pred[512]{0:T(512)(128)(4,1)S(1)} %iota_compare_fusion.2), kind=kOutput, calls=%fused_computation.14.clone.1 | convolution fusion | flops 272891904 | bytes 8921600 | tf_op jit(solution)/shard_map/while/body/eval_jaxpr/while/body/eval_jaxpr/hqk,khe->qhe/dot_general | solution.py:43
  67.4 1.1 dynamic-slice_bitcast_fusion.3
  68.5 6.9 %fusion.166 = (f32[4,512]{1,0:T(4,128)S(1)}, f32[4,512,1024]{2,1,0:T(8,128)}) fusion(pred[512,1024]{1,0:T(8,128)(4,1)S(1)} %fusion.165, bf16[512,4,64]{0,2,1:T(8,128)(2,1)S(1)} %get-tuple-element.195, bf16[2,512,4,64]{1,3,2,0:T(8,128)(2,1)} %get-tuple-element.217, s32[]{:T(128)} %get-tuple-element.206), kind=kOutput, calls=%fused_computation.171.clone.1 | convolution fusion | flops 276825088 | bytes 9445888 | tf_op jit(solution)/shard_map/while/body/eval_jaxpr/while/body/eval_jaxpr/sub | solution.py:41
  76.1 4.9 %fusion.167 = bf16[4,64,512]{2,1,0:T(8,128)(2,1)S(1)} fusion(f32[4,512,1024]{2,1,0:T(8,128)} %get-tuple-element.196, f32[4,512]{1,0:T(4,128)S(1)} %get-tuple-element.197, bf16[512,4,64]{0,2,1:T(8,128)(2,1)S(1)} %get-tuple-element.198, pred[512]{0:T(512)(128)(4,1)S(1)} %iota_compare_fusion.2), kind=kOutput, calls=%fused_computation.14.clone.1 | convolution fusion | flops 272891904 | bytes 8921600 | tf_op jit(solution)/shard_map/while/body/eval_jaxpr/while/body/eval_jaxpr/hqk,khe->qhe/dot_general | solution.py:43
  81.8 3.2 convolution_convert_fusion
  85.3 58.6 %all-reduce.5.cloned.1.call-done = bf16[2,512,1024]{2,1,0:T(8,128)(2,1)} async-done(((bf16[2,512,1024]{2,1,0:T(8,128)(2,1)}), bf16[2,512,1024]{2,1,0:T(8,128)(2,1)}) %all-reduce.5.cloned.1.call-update) | async-done | bytes 2097168 | tf_op jit(solution)/shard_map/psum | solution.py:91
  143.9 3.1 fusion.54
  148.5 1.2 add_convert_fusion
  149.8 3.4 fusion.103
  153.2 12.5 %fusion.92 = bf16[2,512,1024]{2,1,0:T(8,128)(2,1)} fusion(bf16[1024,1024]{1,0:T(8,128)(2,1)S(1)} %copy-done.13, f32[2,512,1024]{2,1,0:T(8,128)S(1)} %get-tuple-element.149, f32[1024]{0:T(1024)S(1)} %copy-done.14, u8[512,1024]{1,0:T(8,128)(4,1)S(1)} %get-tuple-element.123, u8[512,1024]{1,0:T(8,128)(4,1)S(1)} %get-tuple-element.122), kind=kOutput, calls=%fused_computation.105 | convolution fusion | flops 2222981120 | bytes 9441280 | tf_op jit(solution)/shard_map/tsf,fd->tsd/dot_general | solution.py:100
  165.7 55.1 %all-gather = s32[128,2,16]{2,1,0:T(2,128)S(1)} all-gather(s32[1,2,16]{2,1,0:T(2,128)S(1)} %bitcast.89), channel_id=1, replica_groups=mesh['req'=32,'tp'=4] {'req','tp'}, dimensions={0}, use_global_device_ids=true | all-gather | bytes 16512 | tf_op jit(solution)/shard_map/all_gather | solution.py:118
  221.7 25.4 %gather_fusion = bf16[4096,1024]{1,0:T(8,128)(2,1)} fusion(bf16[4096,1024]{1,0:T(8,128)(2,1)} %param.32, s32[4096]{0:T(1024)S(1)} %broadcast_clamp_fusion), kind=kCustom, calls=%fused_computation | custom fusion | bytes 16793600 | tf_op jit(solution)/shard_map/jit(_take)/gather | solution.py:129
  247.2 1.5 fusion.104
  248.6 1.5 multiply_reduce_fusion.1
  250.2 2.4 select_reduce_fusion
  252.6 8.4 %psum.15 = f32[2,1024]{1,0:T(2,128)S(1)} all-reduce(f32[2,1024]{1,0:T(2,128)S(1)} %get-tuple-element.138), channel_id=1, replica_groups=mesh['req'=32,'tp'=4] {'tp'}, use_global_device_ids=true, to_apply=%region_11.12 | all-reduce | flops 2048 | bytes 16384 | tf_op jit(solution)/shard_map/psum | solution.py:112
  261.3 25.0 %all-gather.1 = bf16[32,2,1024]{2,1,0:T(2,128)(2,1)S(1)} all-gather(bf16[1,2,1024]{2,1,0:T(2,128)(2,1)S(1)} %fusion.108), channel_id=1, replica_groups=mesh['req'=32,'tp'=4] {'req'}, dimensions={0}, use_global_device_ids=true | all-gather | bytes 135168 | tf_op jit(solution)/shard_map/all_gather | solution.py:116
  286.4 4.7 %fusion.41 = f32[64,1,64]{2,1,0:T(1,128)S(1)} fusion(bf16[64,1024,1]{1,2,0:T(2,128)(2,1)S(1)} %reshape.275, bf16[64,64,1024]{2,1,0:T(8,128)(2,1)} %bitcast.75, pred[64,64]{1,0:T(8,128)(4,1)S(1)} %compare_and_fusion.1), kind=kOutput, calls=%fused_computation.38 | convolution fusion | flops 12582912 | bytes 8540160 | tf_op jit(solution)/shard_map/td,tcd->tc/dot_general | solution.py:132
  291.4 64.0 %all-reduce.2 = f32[256,16]{1,0:T(8,128)S(1)} all-reduce(f32[256,16]{1,0:T(8,128)S(1)} %bitcast.82), channel_id=3, replica_groups=mesh['req'=32,'tp'=4] {'req','tp'}, use_global_device_ids=true, to_apply=%region_13.14.clone | all-reduce | flops 4096 | bytes 32768
  (83 shorter events, 12.6 us)
Async XLA Ops:
  7.2 142.6 %copy-start = (bf16[1024,1024]{1,0:T(8,128)(2,1)S(1)}, bf16[1024,1024]{1,0:T(8,128)(2,1)}, u32[]{:S(2)}) copy-start(bf16[1024,1024]{1,0:T(8,128)(2,1)} %param.26) | copy-start | bytes 6291460
  7.2 36.5 %all-gather.4.cloned.1.call-start = ((), (), s32[]{:S(2)}) async-start(), calls=%async_computation.1 | async-start | bytes 2621440 | tf_op jit(solution)/shard_map/all_gather | solution.py:75
  7.9 136.0 %all-reduce.5.cloned.1.call-start = ((), (), s32[]{:S(2)}) async-start(), calls=%async_computation.2 | async-start | bytes 4194304 | tf_op jit(solution)/shard_map/psum | solution.py:91
  8.0 40.8 %copy-start.15 = (s32[2]{0:T(128)S(1)}, s32[2]{0:T(128)}, u32[]{:S(2)}) copy-start(s32[2]{0:T(128)} %param.19) | copy-start | bytes 28
  59.6 4.9 %copy-start.4 = (bf16[2,512,256]{1,2,0:T(8,128)(2,1)S(1)}, bf16[2,512,256]{1,2,0:T(8,128)(2,1)}, u32[]{:S(2)}) copy-start(bf16[2,512,256]{1,2,0:T(8,128)(2,1)} %get-tuple-element.207) | copy-start | bytes 1572868 | tf_op jit(solution)/shard_map/while
  64.5 0.8 copy-start.5
  76.0 4.9 %copy-start.4 = (bf16[2,512,256]{1,2,0:T(8,128)(2,1)S(1)}, bf16[2,512,256]{1,2,0:T(8,128)(2,1)}, u32[]{:S(2)}) copy-start(bf16[2,512,256]{1,2,0:T(8,128)(2,1)} %get-tuple-element.207) | copy-start | bytes 1572868 | tf_op jit(solution)/shard_map/while
  81.0 0.8 copy-start.5
  81.8 62.1 %copy-start.7 = (f32[1024]{0:T(1024)S(1)}, f32[1024]{0:T(1024)}, u32[]{:S(2)}) copy-start(f32[1024]{0:T(1024)} %param.23) | copy-start | bytes 12292
  85.1 63.4 %copy-start.10 = (f32[1024]{0:T(1024)S(1)}, f32[1024]{0:T(1024)}, u32[]{:S(2)}) copy-start(f32[1024]{0:T(1024)} %param.25) | copy-start | bytes 12292
  85.1 63.4 %copy-start.11 = (f32[1024]{0:T(1024)S(1)}, f32[1024]{0:T(1024)}, u32[]{:S(2)}) copy-start(f32[1024]{0:T(1024)} %param.24) | copy-start | bytes 12292
  85.1 162.1 %reduce-scatter.2.cloned.1.call-start = ((), (), s32[]{:S(2)}) async-start(), calls=%async_computation.3 | async-start | bytes 2621440 | tf_op jit(solution)/shard_map/reduce_scatter | solution.py:101
  143.9 3.1 copy-start.1
  143.9 3.5 copy-start.2
  148.4 1.3 copy-start.14
  149.8 3.4 copy-start.3
  149.8 3.4 copy-start.13
  153.2 12.5 %copy-start.12 = (s32[2,16]{1,0:T(2,128)S(1)}, s32[2,16]{1,0:T(2,128)}, u32[]{:S(2)}) copy-start(s32[2,16]{1,0:T(2,128)} %param.33) | copy-start | bytes 388
  221.6 25.5 %copy-start.6 = (f32[1024]{0:T(1024)S(1)}, f32[1024]{0:T(1024)}, u32[]{:S(2)}) copy-start(f32[1024]{0:T(1024)} %param.29) | copy-start | bytes 12292
  221.7 28.5 %copy-start.8 = (f32[1024]{0:T(1024)S(1)}, f32[1024]{0:T(1024)}, u32[]{:S(2)}) copy-start(f32[1024]{0:T(1024)} %param.31) | copy-start | bytes 12292
  221.7 28.5 %copy-start.9 = (f32[1024]{0:T(1024)S(1)}, f32[1024]{0:T(1024)}, u32[]{:S(2)}) copy-start(f32[1024]{0:T(1024)} %param.30) | copy-start | bytes 12292
Sparse Core Ops, SparseCore 0:
  9.7 34.0 all-gather.3
  85.2 58.6 all-reduce.4
  165.8 29.5 reduce-scatter.1
where the time goes:
time: 363 us
  blocking collectives  153 us (42%)
  waiting for transfers between devices  95 us (26%)
  matrix products  51.4 us (14%)
  local copies, waits for them, and re-layouts  33.3 us (9%)
  other arithmetic  15.6 us (4%)
  between operations  14.1 us (4%)
    unnamed x1, blocking collectives  64 us
    psum x1, waiting for transfers between devices, per_device(): lax.psum(partial_value.astype(jnp.bfloat16), 'tp').astype(jnp.float32)  58.6 us
    all_gather x1, blocking collectives, per_device(): gathered_ids = lax.all_gather(cand_ids, ('req', 'tp'), axis=0, tiled=True)  55.1 us
    all_gather x1, waiting for transfers between devices, per_device(): full_states = lax.all_gather(states, 'tp', axis=1, tiled=True)  35.7 us
    gather x1, local copies, waits for them, and re-layouts, per_device(): jnp.take(index_rows, safe_ids.reshape(-1), axis=0)  25.4 us
    all_gather x1, blocking collectives, per_device(): all_queries = lax.all_gather(query_vec, 'req', axis=0, tiled=True)  25 us
    sub x2, matrix products, one_block(): expo = jnp.exp(logits - top_val)  13.8 us
    dot_general x1, matrix products, per_device(): jnp.einsum('tsf,fd->tsd', up_act, w_down, preferred_element_type=jnp.floa...  12.5 us
  transfers between devices with their start and end apart: 3, of which 2 were waited for; matrix products, arithmetic and copies ran while one was open for 7% of the time, Pallas kernels for 0%

commit v1 on v0

--- a/solution.py
+++ b/solution.py
@@ -7,6 +7,12 @@
 WINDOW = 512
 layer_eps = 1e-05
 norm_eps = 1e-06
+
+
+def gather_from_all(x, axis, dim):
+    length = lax.axis_size(axis)
+    repeats = [length if d == dim else 1 for d in range(x.ndim)]
+    return lax.all_to_all(jnp.tile(x, repeats), axis, split_axis=dim, concat_axis=dim, tiled=True)
 
 
 def layer_norm(values, gain, shift):
@@ -113,7 +119,7 @@
     query_vec = (
         pooled * lax.rsqrt(jnp.mean(pooled * pooled, axis=-1, keepdims=True) + norm_eps)
     ).astype(jnp.bfloat16)
-    all_queries = lax.all_gather(query_vec, "req", axis=0, tiled=True)
+    all_queries = gather_from_all(query_vec, "req", 0)
     quarter = cand_ids.shape[1]
     gathered_ids = lax.all_gather(cand_ids, ("req", "tp"), axis=0, tiled=True)
     all_ids = (

time: 363 us -> 352 us (0.970)
  blocking collectives: 153 us -> 127 us
  waiting for transfers between devices: 95 us -> 103 us
  starting transfers between devices: 0.3 us -> 6.52 us
    all_gather x1 -> x0, blocking collectives: 25 us -> none  [per_device(): all_queries = lax.all_gather(query_vec, 'req', axis=0, tiled=True)]
    all_to_all x0 -> x1, waiting for transfers between devices: none -> 7.79 us  [gather_from_all(): lax.all_to_all(jnp.tile(x, repeats), axis, split_axis=dim, concat_axis=di...]
    all_to_all x0 -> x1, starting transfers between devices: none -> 6.22 us  [gather_from_all(): lax.all_to_all(jnp.tile(x, repeats), axis, split_axis=dim, concat_axis=di...]
  transfers between devices with their start and end apart: 3 -> 4, of which waited for: 2 -> 3; matrix products, arithmetic and copies ran while one was open for 7% -> 7% of each run, Pallas kernels for 0% -> 0%
where the time goes in v1:
time: 352 us; the launch traced here: 351 us
  blocking collectives  127 us (36%)
  waiting for transfers between devices  103 us (29%)
  matrix products  51.4 us (15%)
  local copies, waits for them, and re-layouts  34.1 us (10%)
  other arithmetic  15.6 us (4%)
  between operations  14.1 us (4%)
  starting transfers between devices  6.52 us (2%)
    unnamed x1, blocking collectives  63 us
    psum x1, waiting for transfers between devices, per_device(): lax.psum(partial_value.astype(jnp.bfloat16), 'tp').astype(jnp.float32)  58.6 us
    all_gather x1, blocking collectives, per_device(): gathered_ids = lax.all_gather(cand_ids, ('req', 'tp'), axis=0, tiled=True)  55.1 us
    all_gather x1, waiting for transfers between devices, per_device(): full_states = lax.all_gather(states, 'tp', axis=1, tiled=True)  35.7 us
    gather x1, local copies, waits for them, and re-layouts, per_device(): jnp.take(index_rows, safe_ids.reshape(-1), axis=0)  25.4 us
    sub x2, matrix products, one_block(): expo = jnp.exp(logits - top_val)  13.8 us
    dot_general x1, matrix products, per_device(): jnp.einsum('tsf,fd->tsd', up_act, w_down, preferred_element_type=jnp.floa...  12.5 us
    dot_general x2, matrix products, one_block(): jnp.einsum('hqk,khe->qhe', attn_weights, values_padded, preferred_element...  9.8 us
  transfers between devices with their start and end apart: 4, of which 3 were waited for; matrix products, arithmetic and copies ran while one was open for 7% of the time, Pallas kernels for 0%

profile of v1, /device:TPU:1, one launch (start us, length us, event | category | flops | bytes accessed | tf_op | source)
XLA Modules:
  0.0 351.2 jit_solution(13242836005155999237)
XLA Ops:
  8.0 35.7 %all-gather.3.cloned.1.call-done = bf16[2,512,1024]{2,1,0:T(8,128)(2,1)} async-done(((bf16[2,128,1024]{2,1,0:T(8,128)(2,1)}), bf16[2,512,1024]{2,1,0:T(8,128)(2,1)}) %all-gather.3.cloned.1.call-update) | async-done | bytes 2097168 | tf_op jit(solution)/shard_map/all_gather | solution.py:81
  43.7 3.9 %add_convert_fusion.1 = bf16[2,512,3,256]{1,3,2,0:T(8,128)(2,1)S(1)} fusion(f32[3,256]{1,0:T(4,128)} %param.21, bf16[1024,3,256]{2,0,1:T(8,128)(2,1)} %param.20, bf16[2,512,1024]{2,1,0:T(8,128)(2,1)} %all-gather.3.cloned.1.call-done), kind=kOutput, calls=%fused_computation.68 | convolution fusion | flops 1612185600 | bytes 5245952 | tf_op jit(solution)/shard_map/tsd,dce->tsce/dot_general | solution.py:86
  47.6 1.2 fusion.149
  48.8 33.0 %while.17 = (s32[]{:T(128)}, bf16[2,512,256]{1,2,0:T(8,128)(2,1)}, s32[2]{0:T(128)S(1)}, bf16[2,512,4,64]{1,3,2,0:T(8,128)(2,1)}, bf16[2,512,4,64]{1,3,2,0:T(8,1...) while((s32[]{:T(128)}, bf16[2,512,256]{1,2,0:T(8,128)(2,1)}, s32[2]{0:T(128)S(1)}, ...), condition=%wide.region_3.4_spmd, body=%wide.region_0.3_spmd.sunk | while | flops 552343040 | bytes 24671904 | solution.py:95
  52.0 6.9 %fusion.165 = (f32[4,512]{1,0:T(4,128)S(1)}, f32[4,512,1024]{2,1,0:T(8,128)}) fusion(pred[512,1024]{1,0:T(8,128)(4,1)S(1)} %fusion.164, bf16[512,4,64]{0,2,1:T(8,128)(2,1)S(1)} %get-tuple-element.195, bf16[2,512,4,64]{1,3,2,0:T(8,128)(2,1)} %get-tuple-element.217, s32[]{:T(128)} %get-tuple-element.206), kind=kOutput, calls=%fused_computation.170.clone.1 | convolution fusion | flops 276825088 | bytes 9445888 | tf_op jit(solution)/shard_map/while/body/eval_jaxpr/while/body/eval_jaxpr/sub | solution.py:47
  59.6 4.9 %fusion.166 = bf16[4,64,512]{2,1,0:T(8,128)(2,1)S(1)} fusion(f32[4,512,1024]{2,1,0:T(8,128)} %get-tuple-element.196, f32[4,512]{1,0:T(4,128)S(1)} %get-tuple-element.197, bf16[512,4,64]{0,2,1:T(8,128)(2,1)S(1)} %get-tuple-element.198, pred[512]{0:T(512)(128)(4,1)S(1)} %iota_compare_fusion.2), kind=kOutput, calls=%fused_computation.14.clone.1 | convolution fusion | flops 272891904 | bytes 8921600 | tf_op jit(solution)/shard_map/while/body/eval_jaxpr/while/body/eval_jaxpr/hqk,khe->qhe/dot_general | solution.py:49
  68.5 6.9 %fusion.165 = (f32[4,512]{1,0:T(4,128)S(1)}, f32[4,512,1024]{2,1,0:T(8,128)}) fusion(pred[512,1024]{1,0:T(8,128)(4,1)S(1)} %fusion.164, bf16[512,4,64]{0,2,1:T(8,128)(2,1)S(1)} %get-tuple-element.195, bf16[2,512,4,64]{1,3,2,0:T(8,128)(2,1)} %get-tuple-element.217, s32[]{:T(128)} %get-tuple-element.206), kind=kOutput, calls=%fused_computation.170.clone.1 | convolution fusion | flops 276825088 | bytes 9445888 | tf_op jit(solution)/shard_map/while/body/eval_jaxpr/while/body/eval_jaxpr/sub | solution.py:47
  76.1 4.9 %fusion.166 = bf16[4,64,512]{2,1,0:T(8,128)(2,1)S(1)} fusion(f32[4,512,1024]{2,1,0:T(8,128)} %get-tuple-element.196, f32[4,512]{1,0:T(4,128)S(1)} %get-tuple-element.197, bf16[512,4,64]{0,2,1:T(8,128)(2,1)S(1)} %get-tuple-element.198, pred[512]{0:T(512)(128)(4,1)S(1)} %iota_compare_fusion.2), kind=kOutput, calls=%fused_computation.14.clone.1 | convolution fusion | flops 272891904 | bytes 8921600 | tf_op jit(solution)/shard_map/while/body/eval_jaxpr/while/body/eval_jaxpr/hqk,khe->qhe/dot_general | solution.py:49
  81.8 3.2 convolution_convert_fusion
  85.3 58.6 %all-reduce.5.cloned.1.call-done = bf16[2,512,1024]{2,1,0:T(8,128)(2,1)} async-done(((bf16[2,512,1024]{2,1,0:T(8,128)(2,1)}), bf16[2,512,1024]{2,1,0:T(8,128)(2,1)}) %all-reduce.5.cloned.1.call-update) | async-done | bytes 2097168 | tf_op jit(solution)/shard_map/psum | solution.py:97
  143.9 3.1 fusion.54
  148.5 1.2 add_convert_fusion
  149.8 3.4 fusion.103
  153.2 12.5 %fusion.92 = bf16[2,512,1024]{2,1,0:T(8,128)(2,1)} fusion(bf16[1024,1024]{1,0:T(8,128)(2,1)S(1)} %copy-done.13, f32[2,512,1024]{2,1,0:T(8,128)S(1)} %get-tuple-element.149, f32[1024]{0:T(1024)S(1)} %copy-done.14, u8[512,1024]{1,0:T(8,128)(4,1)S(1)} %get-tuple-element.123, u8[512,1024]{1,0:T(8,128)(4,1)S(1)} %get-tuple-element.122), kind=kOutput, calls=%fused_computation.105 | convolution fusion | flops 2222981120 | bytes 9441280 | tf_op jit(solution)/shard_map/tsf,fd->tsd/dot_general | solution.py:106
  165.7 55.1 %all-gather = s32[128,2,16]{2,1,0:T(2,128)S(1)} all-gather(s32[1,2,16]{2,1,0:T(2,128)S(1)} %bitcast.87), channel_id=1, replica_groups=mesh['req'=32,'tp'=4] {'req','tp'}, dimensions={0}, use_global_device_ids=true | all-gather | bytes 16512 | tf_op jit(solution)/shard_map/all_gather | solution.py:124
  221.7 25.4 %gather_fusion = bf16[4096,1024]{1,0:T(8,128)(2,1)} fusion(bf16[4096,1024]{1,0:T(8,128)(2,1)} %param.32, s32[4096]{0:T(1024)S(1)} %broadcast_clamp_fusion), kind=kCustom, calls=%fused_computation | custom fusion | bytes 16793600 | tf_op jit(solution)/shard_map/jit(_take)/gather | solution.py:135
  247.1 1.4 fusion.104
  248.6 1.5 multiply_reduce_fusion.1
  250.1 2.4 select_reduce_fusion
  252.5 8.4 %psum.15 = f32[2,1024]{1,0:T(2,128)S(1)} all-reduce(f32[2,1024]{1,0:T(2,128)S(1)} %get-tuple-element.138), channel_id=1, replica_groups=mesh['req'=32,'tp'=4] {'tp'}, use_global_device_ids=true, to_apply=%region_11.12 | all-reduce | flops 2048 | bytes 16384 | tf_op jit(solution)/shard_map/psum | solution.py:118
  262.0 6.2 %all-to-all-start = ((bf16[32,2,1024]{2,1,0:T(2,128)(2,1)}), bf16[32,2,1024]{2,1,0:T(2,128)(2,1)S(1)}, u32[]{:S(2)}, u32[]{:S(2)}) async-start(bf16[32,2,1024]{2,1,0:T(2,128)(2,1)} %tile.2), calls=%async_computation.1 | async-start | bytes 262144 | tf_op jit(solution)/shard_map/all_to_all | solution.py:15
  268.3 7.8 %all-to-all-done = bf16[32,2,1024]{2,1,0:T(2,128)(2,1)S(1)} async-done(((bf16[32,2,1024]{2,1,0:T(2,128)(2,1)}), bf16[32,2,1024]{2,1,0:T(2,128)(2,1)S(1)}, u32[]{:S(2)}, u32[]{:S(2)}) %all-to-all-start) | async-done | bytes 131104 | tf_op jit(solution)/shard_map/all_to_all | solution.py:15
  276.1 4.7 %fusion.41 = f32[64,1,64]{2,1,0:T(1,128)S(1)} fusion(bf16[64,1024,1]{1,2,0:T(2,128)(2,1)S(1)} %reshape.280, bf16[64,64,1024]{2,1,0:T(8,128)(2,1)} %bitcast.73, pred[64,64]{1,0:T(8,128)(4,1)S(1)} %compare_and_fusion.1), kind=kOutput, calls=%fused_computation.38 | convolution fusion | flops 12582912 | bytes 8540160 | tf_op jit(solution)/shard_map/td,tcd->tc/dot_general | solution.py:138
  281.1 63.0 %all-reduce.2 = f32[256,16]{1,0:T(8,128)S(1)} all-reduce(f32[256,16]{1,0:T(8,128)S(1)} %bitcast.80), channel_id=3, replica_groups=mesh['req'=32,'tp'=4] {'req','tp'}, use_global_device_ids=true, to_apply=%region_13.14.clone | all-reduce | flops 4096 | bytes 32768
  (85 shorter events, 14.4 us)
Async XLA Ops:
  7.2 142.6 %copy-start = (bf16[1024,1024]{1,0:T(8,128)(2,1)S(1)}, bf16[1024,1024]{1,0:T(8,128)(2,1)}, u32[]{:S(2)}) copy-start(bf16[1024,1024]{1,0:T(8,128)(2,1)} %param.26) | copy-start | bytes 6291460
  7.2 36.5 %all-gather.3.cloned.1.call-start = ((), (), s32[]{:S(2)}) async-start(), calls=%async_computation.2 | async-start | bytes 2621440 | tf_op jit(solution)/shard_map/all_gather | solution.py:81
  7.9 136.0 %all-reduce.5.cloned.1.call-start = ((), (), s32[]{:S(2)}) async-start(), calls=%async_computation.3 | async-start | bytes 4194304 | tf_op jit(solution)/shard_map/psum | solution.py:97
  8.0 40.8 %copy-start.15 = (s32[2]{0:T(128)S(1)}, s32[2]{0:T(128)}, u32[]{:S(2)}) copy-start(s32[2]{0:T(128)} %param.19) | copy-start | bytes 28
  59.6 4.9 %copy-start.4 = (bf16[2,512,256]{1,2,0:T(8,128)(2,1)S(1)}, bf16[2,512,256]{1,2,0:T(8,128)(2,1)}, u32[]{:S(2)}) copy-start(bf16[2,512,256]{1,2,0:T(8,128)(2,1)} %get-tuple-element.207) | copy-start | bytes 1572868 | tf_op jit(solution)/shard_map/while
  64.5 0.8 copy-start.5
  76.0 4.9 %copy-start.4 = (bf16[2,512,256]{1,2,0:T(8,128)(2,1)S(1)}, bf16[2,512,256]{1,2,0:T(8,128)(2,1)}, u32[]{:S(2)}) copy-start(bf16[2,512,256]{1,2,0:T(8,128)(2,1)} %get-tuple-element.207) | copy-start | bytes 1572868 | tf_op jit(solution)/shard_map/while
  81.0 0.8 copy-start.5
  81.8 62.1 %copy-start.7 = (f32[1024]{0:T(1024)S(1)}, f32[1024]{0:T(1024)}, u32[]{:S(2)}) copy-start(f32[1024]{0:T(1024)} %param.23) | copy-start | bytes 12292
  85.1 63.4 %copy-start.10 = (f32[1024]{0:T(1024)S(1)}, f32[1024]{0:T(1024)}, u32[]{:S(2)}) copy-start(f32[1024]{0:T(1024)} %param.25) | copy-start | bytes 12292
  85.1 63.4 %copy-start.11 = (f32[1024]{0:T(1024)S(1)}, f32[1024]{0:T(1024)}, u32[]{:S(2)}) copy-start(f32[1024]{0:T(1024)} %param.24) | copy-start | bytes 12292
  85.1 162.0 %reduce-scatter.2.cloned.1.call-start = ((), (), s32[]{:S(2)}) async-start(), calls=%async_computation.4 | async-start | bytes 2621440 | tf_op jit(solution)/shard_map/reduce_scatter | solution.py:107
  143.9 3.1 copy-start.1
  143.9 3.5 copy-start.2
  148.4 1.3 copy-start.14
  149.8 3.4 copy-start.3
  149.8 3.4 copy-start.13
  153.2 12.5 %copy-start.12 = (s32[2,16]{1,0:T(2,128)S(1)}, s32[2,16]{1,0:T(2,128)}, u32[]{:S(2)}) copy-start(s32[2,16]{1,0:T(2,128)} %param.33) | copy-start | bytes 388
  221.6 25.5 %copy-start.6 = (f32[1024]{0:T(1024)S(1)}, f32[1024]{0:T(1024)}, u32[]{:S(2)}) copy-start(f32[1024]{0:T(1024)} %param.29) | copy-start | bytes 12292
  221.7 28.5 %copy-start.8 = (f32[1024]{0:T(1024)S(1)}, f32[1024]{0:T(1024)}, u32[]{:S(2)}) copy-start(f32[1024]{0:T(1024)} %param.31) | copy-start | bytes 12292
  221.7 28.5 %copy-start.9 = (f32[1024]{0:T(1024)S(1)}, f32[1024]{0:T(1024)}, u32[]{:S(2)}) copy-start(f32[1024]{0:T(1024)} %param.30) | copy-start | bytes 12292
  262.0 14.0 %all-to-all-start = ((bf16[32,2,1024]{2,1,0:T(2,128)(2,1)}), bf16[32,2,1024]{2,1,0:T(2,128)(2,1)S(1)}, u32[]{:S(2)}, u32[]{:S(2)}) async-start(bf16[32,2,1024]{2,1,0:T(2,128)(2,1)} %tile.2), calls=%async_computation.1 | async-start | bytes 262144 | tf_op jit(solution)/shard_map/all_to_all | solution.py:15
Sparse Core Ops, SparseCore 0:
  9.7 34.0 all-gather.2
  85.2 58.6 all-reduce.4
  165.8 29.5 reduce-scatter.1
